TPU v7x, 256 devices: a whole 4x4x8 slice. The times are simulated.
256 devices in a mesh: row: 16 (over z, core), col: 8 (over x, y_lo), vec: 2 (over y_hi).
Axes of the slice: x: 4, y: 4 (y_hi: 2, y_lo: 2; y = y_hi * 2 + y_lo), z: 8, core: 2. Of those that a mesh axis runs over, the one named last changes fastest.
Arguments:
- vectors: bfloat16 [16, 131072], P('vec', ('row', 'col')), may hold values from -6 to 6
- tile_vals: bfloat16 [16, 8, 256, 128, 128], P('row', 'col'), may hold values from -0.09375 to 0.09375
- tile_rows: int32 [16, 8, 256], P('row', 'col'), may hold values from 0 to 1023, as said below
- tile_cols: int32 [16, 8, 256], P('row', 'col'), may hold values from 0 to 1023, as said below
- tile_counts: int32 [16, 8], P('row', 'col'), may hold values from 1 to 256, as said below
Outputs:
- product: bfloat16 [16, 131072], P('vec', ('row', 'col'))
- gram: float32 [16, 16], P(None, 'vec')
Inputs may be any that keep to these rules, and one draw needn't show every extreme that they name: `tile_rows`: list [i, j] names tiles whose row index r has i * 64 <= r < (i + 1) * 64 and whose column index c has (c // 8) % (8) == j, that is the column's block of 8 tile rows, numbered c // 8, is held by column group j; live slots name distinct tiles with r >= c; slots at or beyond the count hold in-range indices that must be ignored. `tile_cols`: see tile_rows; the same slots. `tile_counts`: some lists are full in every draw; lists near the top of the triangle hold few tiles.
All inputs are finite; a program needn't handle non-finite values.
Results may differ from a plain program's by a relative error of at most 0.001.
Values may be sent and summed in bfloat16 or wider, within the bound.
A program may use at most 64 MiB of HBM per device.

v0:
```python
import math
import jax
import jax.numpy as jnp
from jax import lax
from jax.sharding import PartitionSpec as P


def shards(vectors, tile_vals, tile_rows, tile_cols, tile_counts):
    nrow = lax.axis_size("row")
    ncol = lax.axis_size("col")
    vlocal, width = vectors.shape
    tile = tile_vals.shape[-1]
    stretch = width // tile
    span = ncol * stretch
    colspan = nrow * stretch
    row_x = lax.all_gather(vectors, "col", axis=1, tiled=True)
    col_x = lax.all_gather(vectors, "row", axis=1, tiled=True)
    tiles = tile_vals[0, 0]
    rows = tile_rows[0, 0]
    cols = tile_cols[0, 0]
    count = tile_counts[0, 0]
    slots = jnp.arange(rows.shape[0], dtype=jnp.int32)
    live = slots < count
    mirror = live & (rows != cols)
    row_place = rows % span
    col_place = cols // span * stretch + cols % stretch
    row_blocks = row_x.reshape(vlocal, span, tile)
    col_blocks = col_x.reshape(vlocal, colspan, tile)
    picked_cols = jnp.take(col_blocks, col_place, axis=1)
    picked_rows = jnp.take(row_blocks, row_place, axis=1)
    down = jnp.einsum("tij,vtj->vti", tiles, picked_cols, preferred_element_type=jnp.float32)
    upper = jnp.einsum("tij,vti->vtj", tiles, picked_rows, preferred_element_type=jnp.float32)
    row_hit = (
        (row_place[None, :] == jnp.arange(span, dtype=jnp.int32)[:, None]) & live[None, :]
    ).astype(jnp.float32)
    col_hit = (
        (col_place[None, :] == jnp.arange(colspan, dtype=jnp.int32)[:, None]) & mirror[None, :]
    ).astype(jnp.float32)
    row_part = jnp.einsum("at,vti->vai", row_hit, down, precision=lax.Precision.HIGHEST).reshape(
        vlocal, span * tile
    )
    col_part = jnp.einsum("at,vti->vai", col_hit, upper, precision=lax.Precision.HIGHEST).reshape(
        vlocal, colspan * tile
    )
    row_whole = lax.psum(row_part, "col")
    col_whole = lax.psum(col_part, "row")
    row_share = lax.dynamic_slice_in_dim(row_whole, lax.axis_index("col") * width, width, 1)
    col_share = lax.dynamic_slice_in_dim(col_whole, lax.axis_index("row") * width, width, 1)
    image = row_share + col_share
    every_vector = lax.all_gather(vectors, "vec", axis=0, tiled=True)
    partial_gram = jnp.dot(
        every_vector.astype(jnp.float32), image.T, precision=lax.Precision.HIGHEST
    )
    gram = lax.psum(partial_gram, ("row", "col")) / math.sqrt(width * nrow * ncol)
    return (image.astype(jnp.bfloat16), gram)


def solution(mesh):
    return jax.shard_map(
        shards,
        mesh=mesh,
        in_specs=(
            P("vec", ("row", "col")),
            P("row", "col", None, None, None),
            P("row", "col", None),
            P("row", "col", None),
            P("row", "col"),
        ),
        out_specs=(P("vec", ("row", "col")), P(None, "vec")),
        check_vma=False,
    )
```

profile of v0, /device:TPU:8, one launch (start us, length us, event | category | flops | bytes accessed | tf_op | source)
XLA Modules:
  0.0 527.4 jit_solution(8425430569256399796)
XLA Ops:
  7.2 0.0 copy-start.1
  7.2 0.0 copy-start.2
  7.2 0.0 all-reduce.5.cloned.1.call-start
  7.2 28.5 %all_gather.10 = bf16[8,8192]{1,0:T(8,128)(2,1)S(1)} all-gather(bf16[8,1024]{1,0:T(8,128)(2,1)} %param.5), channel_id=1, replica_groups=mesh['row'=16,'col'=8,'vec'=2] {'col'}, dimensions={1}, use_global_device_ids=true | all-gather | bytes 147456 | tf_op jit(solution)/shard_map/all_gather | solution.py:16
  35.8 0.7 compare_select_fusion
  36.5 0.7 compare_and_fusion.1
  37.2 0.8 gather_fusion.1
  38.0 0.0 copy-start
  38.0 4.7 fusion
  42.7 0.4 copy.9
  43.8 0.0 copy-done.1
  43.8 0.0 copy-done.2
  43.8 0.6 convolution_bitcast_fusion
  44.5 0.2 copy.7
  44.7 1.1 copy.18
  45.8 0.0 all-reduce.5.cloned.1.call-update
  45.8 0.0 all-reduce.3.cloned.1.call-start
  45.9 0.0 copy-done
  45.9 20.7 %all_gather.9 = bf16[8,16384]{1,0:T(8,128)(2,1)S(1)} all-gather(bf16[8,1024]{1,0:T(8,128)(2,1)S(1)} %copy-done), channel_id=1, replica_groups=mesh['row'=16,'col'=8,'vec'=2] {'row'}, dimensions={1}, use_global_device_ids=true | all-gather | bytes 278528 | tf_op jit(solution)/shard_map/all_gather | solution.py:17
  66.6 0.8 gather_fusion
  67.4 6.8 %fusion.2 = f32[256,8,128]{2,1,0:T(8,128)S(1)} fusion(bf16[1,1,256,128,128]{4,3,2,1,0:T(8,128)(2,1)} %param.6, bf16[256,8,128]{2,1,0:T(8,128)(2,1)S(1)} %gather_fusion, pred[256]{0:T(512)(128)(4,1)S(1)} %get-tuple-element.2), kind=kOutput, calls=%fused_computation.4 | convolution fusion | flops 67371008 | bytes 9961728 | tf_op jit(solution)/shard_map/tij,vtj->vti/dot_general | solution.py:31
  74.2 0.6 convolution_bitcast_fusion.1
  74.8 0.9 copy.19
  75.7 0.0 all-reduce.3.cloned.1.call-update
  75.7 5.9 %all_gather.11 = bf16[16,1024]{1,0:T(8,128)(2,1)S(1)} all-gather(bf16[8,1024]{1,0:T(8,128)(2,1)S(1)} %copy-done), channel_id=1, replica_groups=mesh['row'=16,'col'=8,'vec'=2] {'vec'}, dimensions={0}, use_global_device_ids=true | all-gather | bytes 49152 | tf_op jit(solution)/shard_map/all_gather | solution.py:50
  81.7 77.3 %all-reduce.5.cloned.1.call-done = f32[8,16384]{1,0:T(8,128)} async-done(((f32[8,16384]{1,0:T(8,128)}), f32[8,16384]{1,0:T(8,128)}) %all-reduce.5.cloned.1.call-update) | async-done | bytes 524304 | tf_op jit(solution)/shard_map/psum | solution.py:46
  159.0 79.9 %all-reduce.3.cloned.1.call-done = f32[8,8192]{1,0:T(8,128)} async-done(((f32[8,8192]{1,0:T(8,128)}), f32[8,8192]{1,0:T(8,128)}) %all-reduce.3.cloned.1.call-update) | async-done | bytes 262160 | tf_op jit(solution)/shard_map/psum | solution.py:45
  238.9 0.9 convolution_bitcast_fusion.2
  239.8 278.8 %psum.23 = f32[16,8]{0,1:T(8,128)S(1)} all-reduce(f32[16,8]{0,1:T(8,128)S(1)} %convolution_bitcast_fusion.2), channel_id=1, replica_groups=mesh['row'=16,'col'=8,'vec'=2] {'row','col'}, use_global_device_ids=true, to_apply=%region_2.3 | all-reduce | flops 128 | bytes 1024 | tf_op jit(solution)/shard_map/psum | solution.py:54
  518.6 0.6 broadcast_multiply_fusion
  519.2 1.4 fusion.25
  (5 shorter events, 0.1 us)
Async XLA Ops:
  7.2 36.6 %copy-start.1 = (s32[1,1,256]{2,1,0:T(1,128)S(1)}, s32[1,1,256]{2,1,0:T(1,128)}, u32[]{:S(2)}) copy-start(s32[1,1,256]{2,1,0:T(1,128)} %param.7) | copy-start | bytes 3076
  7.2 36.6 %copy-start.2 = (s32[1,1,256]{2,1,0:T(1,128)S(1)}, s32[1,1,256]{2,1,0:T(1,128)}, u32[]{:S(2)}) copy-start(s32[1,1,256]{2,1,0:T(1,128)} %param.8) | copy-start | bytes 3076
  7.2 151.8 %all-reduce.5.cloned.1.call-start = ((), (), s32[]{:S(2)}) async-start(), calls=%async_computation.1 | async-start | bytes 1048576 | tf_op jit(solution)/shard_map/psum | solution.py:46
  38.0 7.9 %copy-start = (bf16[8,1024]{1,0:T(8,128)(2,1)S(1)}, bf16[8,1024]{1,0:T(8,128)(2,1)}, u32[]{:S(2)}) copy-start(bf16[8,1024]{1,0:T(8,128)(2,1)} %param.5) | copy-start | bytes 49156
  45.8 193.1 %all-reduce.3.cloned.1.call-start = ((), (), s32[]{:S(2)}) async-start(), calls=%async_computation | async-start | bytes 524288 | tf_op jit(solution)/shard_map/psum | solution.py:45
Sparse Core Ops, SparseCore 0:
  45.9 113.0 all-reduce.4
  161.6 77.2 all-reduce.2
where the time goes:
time: 528 us; the launch traced here: 527 us
  blocking collectives  334 us (63%)
  waiting for transfers between devices  157 us (30%)
  between operations  14.8 us (3%)
  matrix products  13.7 us (3%)
    psum x1, blocking collectives, shards(): lax.psum(partial_gram, ('row', 'col')) / math.sqrt(width * nrow * ncol)  279 us
    psum x1, waiting for transfers between devices, shards(): row_whole = lax.psum(row_part, 'col')  79.9 us
    psum x1, waiting for transfers between devices, shards(): col_whole = lax.psum(col_part, 'row')  77.3 us
    all_gather x1, blocking collectives, shards(): row_x = lax.all_gather(vectors, 'col', axis=1, tiled=True)  28.5 us
    all_gather x1, blocking collectives, shards(): col_x = lax.all_gather(vectors, 'row', axis=1, tiled=True)  20.7 us
  transfers between devices with their start and end apart: 2, of which 2 were waited for; matrix products, arithmetic and copies ran while one was open for 2% of the time, Pallas kernels for 0%

commit v1 on v0

--- a/solution.py
+++ b/solution.py
@@ -13,7 +13,9 @@
     stretch = width // tile
     span = ncol * stretch
     colspan = nrow * stretch
-    row_x = lax.all_gather(vectors, "col", axis=1, tiled=True)
+    row_x = jnp.concatenate(
+        lax.all_to_all(jnp.stack([vectors] * lax.axis_size("col")), "col", 0, 0), axis=1
+    )
     col_x = lax.all_gather(vectors, "row", axis=1, tiled=True)
     tiles = tile_vals[0, 0]
     rows = tile_rows[0, 0]

time: 528 us -> 527 us (level)
  blocking collectives: 334 us -> 304 us
  waiting for transfers between devices: 157 us -> 175 us
  starting transfers between devices: 0.08 us -> 5.8 us
    psum x1, waiting for transfers between devices: 77.3 us -> 115 us  [shards(): col_whole = lax.psum(col_part, 'row')]
    all_gather x1 -> x0, blocking collectives: 28.5 us -> none  [shards(): row_x = lax.all_gather(vectors, 'col', axis=1, tiled=True)]
    psum x1, waiting for transfers between devices: 79.9 us -> 60.8 us  [shards(): row_whole = lax.psum(row_part, 'col')]
    all_to_all x0 -> x1, starting transfers between devices: none -> 5.76 us  [shards(): lax.all_to_all(jnp.stack([vectors] * lax.axis_size('col')), 'col', 0, 0)]
  transfers between devices with their start and end apart: 2 -> 3, of which waited for: 2 -> 2; matrix products, arithmetic and copies ran while one was open for 2% -> 4% of each run, Pallas kernels for 0% -> 0%
where the time goes in v1:
time: 527 us; the launch traced here: 522 us
  blocking collectives  304 us (58%)
  waiting for transfers between devices  175 us (33%)
  between operations  14.8 us (3%)
  matrix products  14.1 us (3%)
  starting transfers between devices  5.8 us (1%)
    psum x1, blocking collectives, shards(): lax.psum(partial_gram, ('row', 'col')) / math.sqrt(width * nrow * ncol)  277 us
    psum x1, waiting for transfers between devices, shards(): col_whole = lax.psum(col_part, 'row')  115 us
    psum x1, waiting for transfers between devices, shards(): row_whole = lax.psum(row_part, 'col')  60.8 us
    all_gather x1, blocking collectives, shards(): col_x = lax.all_gather(vectors, 'row', axis=1, tiled=True)  20.9 us
  transfers between devices with their start and end apart: 3, of which 2 were waited for; matrix products, arithmetic and copies ran while one was open for 4% of the time, Pallas kernels for 0%

profile of v1, /device:TPU:8, one launch (start us, length us, event | category | flops | bytes accessed | tf_op | source)
XLA Modules:
  0.0 522.3 jit_solution(1593550357228074085)
XLA Ops:
  7.2 0.0 copy-start.1
  7.2 1.4 stack.2
  8.6 5.8 %all-to-all-start = ((bf16[8,8,1024]{2,1,0:T(8,128)(2,1)}), bf16[8,8,1024]{2,1,0:T(8,128)(2,1)S(1)}, u32[]{:S(2)}, u32[]{:S(2)}) async-start(bf16[8,8,1024]{2,1,0:T(8,128)(2,1)} %stack.2), calls=%async_computation | async-start | bytes 262144 | tf_op jit(solution)/shard_map/all_to_all | solution.py:17
  14.3 0.0 all-reduce.3.cloned.1.call-start
  14.3 20.9 %all_gather.6 = bf16[8,16384]{1,0:T(8,128)(2,1)S(1)} all-gather(bf16[8,1024]{1,0:T(8,128)(2,1)} %param.5), channel_id=1, replica_groups=mesh['row'=16,'col'=8,'vec'=2] {'row'}, dimensions={1}, use_global_device_ids=true | all-gather | bytes 278528 | tf_op jit(solution)/shard_map/all_gather | solution.py:19
  35.9 0.7 compare_select_fusion.1
  36.6 0.8 gather_fusion
  37.4 0.7 compare_and_fusion.1
  38.1 6.8 %fusion.4 = f32[8,256,128]{2,0,1:T(8,128)S(1)} fusion(bf16[1,1,256,128,128]{4,3,2,1,0:T(8,128)(2,1)} %param.6, bf16[256,8,128]{2,1,0:T(8,128)(2,1)S(1)} %gather_fusion, pred[256]{0:T(512)(128)(4,1)S(1)} %get-tuple-element.8), kind=kOutput, calls=%fused_computation.6 | convolution fusion | flops 67371008 | bytes 9961728 | tf_op jit(solution)/shard_map/tij,vtj->vti/dot_general | solution.py:33
  45.0 0.0 copy-start
  45.0 0.6 convolution_bitcast_fusion.1
  45.6 0.9 copy.23
  46.4 0.0 all-reduce.3.cloned.1.call-update
  46.5 0.0 all-reduce.5.cloned.1.call-start
  46.5 0.0 copy-done.1
  46.6 0.0 all-to-all-done
  46.6 0.8 gather_fusion.1
  47.4 4.7 fusion.7
  52.1 1.0 convolution_bitcast_fusion
  53.2 0.2 copy.13
  53.4 1.1 copy.22
  54.5 0.0 all-reduce.5.cloned.1.call-update
  54.5 0.0 copy-done
  54.5 6.0 %all_gather.7 = bf16[16,1024]{1,0:T(8,128)(2,1)S(1)} all-gather(bf16[8,1024]{1,0:T(8,128)(2,1)S(1)} %copy-done), channel_id=1, replica_groups=mesh['row'=16,'col'=8,'vec'=2] {'vec'}, dimensions={0}, use_global_device_ids=true | all-gather | bytes 49152 | tf_op jit(solution)/shard_map/all_gather | solution.py:52
  60.6 60.8 %all-reduce.3.cloned.1.call-done = f32[8,8192]{1,0:T(8,128)} async-done(((f32[8,8192]{1,0:T(8,128)}), f32[8,8192]{1,0:T(8,128)}) %all-reduce.3.cloned.1.call-update) | async-done | bytes 262160 | tf_op jit(solution)/shard_map/psum | solution.py:47
  121.4 114.5 %all-reduce.5.cloned.1.call-done = f32[8,16384]{1,0:T(8,128)} async-done(((f32[8,16384]{1,0:T(8,128)}), f32[8,16384]{1,0:T(8,128)}) %all-reduce.5.cloned.1.call-update) | async-done | bytes 524304 | tf_op jit(solution)/shard_map/psum | solution.py:48
  235.9 0.9 convolution_bitcast_fusion.2
  236.8 276.7 %psum.23 = f32[16,8]{0,1:T(8,128)S(1)} all-reduce(f32[16,8]{0,1:T(8,128)S(1)} %convolution_bitcast_fusion.2), channel_id=1, replica_groups=mesh['row'=16,'col'=8,'vec'=2] {'row','col'}, use_global_device_ids=true, to_apply=%region_2.3 | all-reduce | flops 128 | bytes 1024 | tf_op jit(solution)/shard_map/psum | solution.py:56
  513.5 0.6 broadcast_multiply_fusion
  514.1 1.4 fusion.30
  (4 shorter events, 0.0 us)
Async XLA Ops:
  7.2 39.4 %copy-start.1 = (s32[1,1,256]{2,1,0:T(1,128)S(1)}, s32[1,1,256]{2,1,0:T(1,128)}, u32[]{:S(2)}) copy-start(s32[1,1,256]{2,1,0:T(1,128)} %param.7) | copy-start | bytes 3076
  8.6 38.0 %all-to-all-start = ((bf16[8,8,1024]{2,1,0:T(8,128)(2,1)}), bf16[8,8,1024]{2,1,0:T(8,128)(2,1)S(1)}, u32[]{:S(2)}, u32[]{:S(2)}) async-start(bf16[8,8,1024]{2,1,0:T(8,128)(2,1)} %stack.2), calls=%async_computation | async-start | bytes 262144 | tf_op jit(solution)/shard_map/all_to_all | solution.py:17
  14.3 107.1 %all-reduce.3.cloned.1.call-start = ((), (), s32[]{:S(2)}) async-start(), calls=%async_computation.1 | async-start | bytes 524288 | tf_op jit(solution)/shard_map/psum | solution.py:47
  45.0 9.6 %copy-start = (bf16[8,1024]{1,0:T(8,128)(2,1)S(1)}, bf16[8,1024]{1,0:T(8,128)(2,1)}, u32[]{:S(2)}) copy-start(bf16[8,1024]{1,0:T(8,128)(2,1)} %param.5) | copy-start | bytes 49156
  46.5 189.4 %all-reduce.5.cloned.1.call-start = ((), (), s32[]{:S(2)}) async-start(), calls=%async_computation.2 | async-start | bytes 1048576 | tf_op jit(solution)/shard_map/psum | solution.py:48
Sparse Core Ops, SparseCore 0:
  46.6 74.7 all-reduce.2
  123.7 112.1 all-reduce.4
